TPU v7x, 128 devices: a whole 4x4x4 slice. The times are simulated.
128 devices in a mesh: tm: 16 (over z, y), member: 8 (over x, core).
Axes of the slice: x: 4, y: 4, z: 4, core: 2. Of those that a mesh axis runs over, the one named last changes fastest.
Arguments:
- queries: bfloat16 [65536, 512], P(('member', 'tm')), parts along dimension 0, may hold values from -12 to 12
- key_rows: bfloat16 [65536, 512], P(('member', 'tm')), parts along dimension 0, may hold values from -6 to 6
- value_rows: bfloat16 [65536, 512], P(('member', 'tm')), parts along dimension 0, may hold values from -6 to 6
- grad_output: bfloat16 [65536, 512], P(('member', 'tm')), parts along dimension 0, may hold values from -6 to 6
- extra_blocks: int32 [128, 16], P('member'), parts along dimension 0, may hold values from -1 to 511, as said below
Outputs:
- mixed_rows: bfloat16 [65536, 512], P(('member', 'tm')), parts along dimension 0
- query_grad: bfloat16 [65536, 512], P(('member', 'tm')), parts along dimension 0
- key_grad: bfloat16 [65536, 512], P(('member', 'tm')), parts along dimension 0
- value_grad: bfloat16 [65536, 512], P(('member', 'tm')), parts along dimension 0
There are 8 independent parts, one for each index of `member`. A program takes and returns all parts, laid end to end along the dimension named above; each array names one. Nothing has to cross between parts.
Inputs may be any that keep to these rules, and one draw needn't show every extreme that they name: `extra_blocks`: row b lists distinct sub-blocks of 16 rows, each inside an earlier block; -1 marks an empty entry, and empty entries stand after the others. From any one block a row takes either no sub-block or exactly 2.
All inputs are finite; a program needn't handle non-finite values.
Results may differ from a plain program's by a relative error of at most 0.035.
Values may be sent and summed in bfloat16 or wider, within the bound.
A program may use at most 128 MiB of HBM per device.

v0:
```python
import math

import jax
import jax.numpy as jnp
from jax import lax
from jax.experimental import pallas as pl
from jax.experimental.pallas import tpu as pltpu
from jax.sharding import PartitionSpec as P

HD = 64
SUB = 16
CAP = 2
MESH = pl.DeviceIdType.MESH
NT = (((1,), (1,)), ((), ()))
NN = (((1,), (0,)), ((), ()))
TN = (((0,), (0,)), ((), ()))
very_negative = -1e30
f32 = jnp.float32
bf16 = jnp.bfloat16

DEVICES = 16
SIDE = 4
BLOCK = 512
WIDTH = 512
PAIR = 128
GROUPS = WIDTH // PAIR
PER_BLOCK = BLOCK // SUB
DISTANCES = (1, 2, 4, 8)
FAR = tuple(d for d in range(1, DEVICES) if d not in DISTANCES)
SLOT_ROWS = CAP * SUB
EXTRA_ROWS = 384
KEYS = 5 * BLOCK + EXTRA_ROWS
CHUNKS = tuple((i * BLOCK, BLOCK) for i in range(5)) + ((5 * BLOCK, EXTRA_ROWS),)


def dot(a, b, dims):
    return lax.dot_general(a, b, dims, preferred_element_type=f32)


def kernel(
    q, k, v, do, table,
    o, dq, dk, dv,
    rx, xx, xs, tb, own, et, xt, rb, cr, xr,
    s_ref, p_ref, vt, qt, dot_t, bias, spread,
    send_kv, recv_kv, send_relay, send_x, recv_x,
    send_t, recv_t, recv_c, send_xt, recv_xt,
):
    me = lax.axis_index("tm")
    col = lax.rem(me, SIDE)
    row = me // SIDE

    def device(index):
        return {"tm": index}

    barrier = pltpu.get_barrier_semaphore()
    for i in range(DEVICES):
        @pl.when(me != i)
        def _():
            pl.semaphore_signal(barrier, inc=1, device_id=device(i), device_id_type=MESH)
    pl.semaphore_wait(barrier, DEVICES - 1)

    def lanes(g):
        return pl.ds(pl.multiple_of(g * PAIR, PAIR), PAIR)

    def kv_copies(g, level, src_k, src_v, send, to):
        return [
            pltpu.make_async_remote_copy(
                src_ref=src,
                dst_ref=rx.at[g, level, part],
                send_sem=send.at[g, level, part],
                recv_sem=recv_kv.at[g, level, part],
                device_id=device(to),
                device_id_type=MESH,
            )
            for part, src in enumerate((src_k, src_v))
        ]

    def own_copies(g, level, to):
        return kv_copies(g, level, k.at[:, lanes(g)], v.at[:, lanes(g)], send_kv, to)

    def relay_copies(g, level, to):
        return kv_copies(g, level, rx.at[g, 2, 0], rx.at[g, 2, 1], send_relay, to)

    direct = (
        (2, me + 4 < DEVICES),
        (0, (col < 3) & (me + 1 < DEVICES)),
        (1, col < 2),
        (3, me + 8 < DEVICES),
    )
    relays = (
        (0, 3, (col == 3) & (row >= 1)),
        (1, 2, (col >= 2) & (row >= 1)),
    )

    def send_blocks(g):
        for level, cond in direct:
            @pl.when(cond)
            def _():
                for copy in own_copies(g, level, me + DISTANCES[level]):
                    copy.start()

    def wait_blocks(g, level):
        @pl.when(me >= DISTANCES[level])
        def _():
            for copy in own_copies(g, level, me):
                copy.wait_recv()

    def relay_blocks(g):
        wait_blocks(g, 2)
        for level, back, cond in relays:
            @pl.when(cond)
            def _():
                for copy in relay_copies(g, level, me - back):
                    copy.start()

    send_blocks(0)
    send_blocks(1)

    def gap_of(i):
        return i + 3 + (i + 10) // 11 + (i + 7) // 11

    def extra_copy(i, to):
        rows = pl.ds(pl.multiple_of(i * SLOT_ROWS, SLOT_ROWS), SLOT_ROWS)
        return pltpu.make_async_remote_copy(
            src_ref=xs.at[:, :, rows, :],
            dst_ref=xx.at[:, :, rows, :],
            send_sem=send_x.at[i],
            recv_sem=recv_x.at[i],
            device_id=device(to),
            device_id_type=MESH,
        )

    spread[...] = jnp.zeros_like(spread)

    def find(i, _):
        other = me + gap_of(i)

        @pl.when(other < DEVICES)
        def _():
            first = me * PER_BLOCK
            count = jnp.int32(0)
            index = [jnp.int32(0), jnp.int32(0)]
            for n in range(table.shape[1]):
                entry = table[other, n]
                inside = entry - first
                mine = (inside >= 0) & (inside < PER_BLOCK)
                for slot in range(CAP):
                    index[slot] = jnp.where(mine & (count == slot), inside, index[slot])
                count = count + jnp.where(mine, 1, 0)
            for slot in range(CAP):
                base = jnp.where(count > slot, index[slot] * SUB, jnp.int32(-4096))
                hit = lax.broadcasted_iota(jnp.int32, (SUB, BLOCK), 1) == (
                    lax.broadcasted_iota(jnp.int32, (SUB, BLOCK), 0) + base
                )
                spread[pl.ds(pl.multiple_of(i * SLOT_ROWS + slot * SUB, SUB), SUB), :] = jnp.where(
                    hit, 1.0, 0.0
                ).astype(bf16)

        return 0

    lax.fori_loop(0, len(FAR), find, 0)
    for part, ref in enumerate((k, v)):
        for g in range(GROUPS):
            xs[g, part] = dot(spread[...], ref[:, g * PAIR:(g + 1) * PAIR], NN).astype(bf16)

    def extras_leave(i, _):
        @pl.when(me + gap_of(i) < DEVICES)
        def _():
            extra_copy(i, me + gap_of(i)).start()
        return 0

    lax.fori_loop(0, len(FAR), extras_leave, 0)

    key_row = lax.broadcasted_iota(jnp.int32, (8, BLOCK), 1)
    for level, distance in enumerate(DISTANCES):
        sub_block = (me - distance) * PER_BLOCK + (key_row >> 4)
        times = jnp.zeros((8, BLOCK), f32)
        for n in range(table.shape[1]):
            times = times + jnp.where(sub_block == table[me, n], 1.0, 0.0)
        value = jnp.where(times > 0.5, 1.0, 0.0)
        low, size = CHUNKS[1 + level]
        bias[:, low:low + size] = jnp.where(sub_block >= 0, value, very_negative)
    key_row = lax.broadcasted_iota(jnp.int32, (8, EXTRA_ROWS), 1)
    place = key_row >> 5
    owner = me - (place + 3 + jnp.where(place >= 1, 1, 0) + jnp.where(place >= 4, 1, 0))
    times = jnp.zeros((8, EXTRA_ROWS), f32)
    for n in range(table.shape[1]):
        entry = table[me, n]
        inside = entry - owner * PER_BLOCK
        times = times + jnp.where((inside >= 0) & (inside < PER_BLOCK), 1.0, 0.0)
    slot_of = ((key_row >> 4) & 1).astype(f32)
    live = (times > slot_of + 0.5) & (owner >= 0) & (place < len(FAR))
    bias[:, 5 * BLOCK:] = jnp.where(live, 0.0, very_negative)

    for level, distance in enumerate(DISTANCES):
        @pl.when(me < distance)
        def _():
            def clear(g, _):
                rx[g, level] = jnp.zeros(rx.shape[2:], bf16)
                return 0
            lax.fori_loop(0, GROUPS, clear, 0)
    tail = len(FAR) * SLOT_ROWS
    xx[:, :, tail:, :] = jnp.zeros((GROUPS, 2, EXTRA_ROWS - tail, PAIR), bf16)
    xr[:, tail:, :] = jnp.zeros((2 * GROUPS, EXTRA_ROWS - tail, PAIR), bf16)

    def clear_extra(i, _):
        rows = pl.ds(pl.multiple_of(i * SLOT_ROWS, SLOT_ROWS), SLOT_ROWS)

        @pl.when(me - gap_of(i) < 0)
        def _():
            xx[:, :, rows, :] = jnp.zeros((GROUPS, 2, SLOT_ROWS, PAIR), bf16)

        @pl.when(me + gap_of(i) >= DEVICES)
        def _():
            xr[:, rows, :] = jnp.zeros((2 * GROUPS, SLOT_ROWS, PAIR), bf16)

        return 0

    lax.fori_loop(0, len(FAR), clear_extra, 0)

    def term_copy(g, level, dst, recv, to):
        return pltpu.make_async_remote_copy(
            src_ref=tb.at[g, level],
            dst_ref=dst,
            send_sem=send_t.at[g, level],
            recv_sem=recv,
            device_id=device(to),
            device_id_type=MESH,
        )

    def term_home(g, level, to):
        return term_copy(g, level, rb.at[g, level], recv_t.at[g, level], to)

    def term_aside(g, level, to):
        return term_copy(g, level, cr.at[g, level], recv_c.at[g, level], to)

    def extra_term(g, i, to):
        rows = pl.ds(pl.multiple_of(i * SLOT_ROWS, SLOT_ROWS), SLOT_ROWS)
        both = pl.ds(2 * g, 2)
        return pltpu.make_async_remote_copy(
            src_ref=xt.at[both, rows, :],
            dst_ref=xr.at[both, rows, :],
            send_sem=send_xt.at[g, i],
            recv_sem=recv_xt.at[g, i],
            device_id=device(to),
            device_id_type=MESH,
        )

    homes = (
        (0, col >= 1),
        (1, col >= 2),
        (3, me >= 8),
        (2, (col < 2) & (row >= 1)),
    )
    asides = (
        (0, 3, (col == 0) & (row >= 1)),
        (1, 2, (col < 2) & (row >= 1)),
    )
    mixes = (
        (0, (col == 3) & (row >= 1)),
        (1, (col >= 2) & (row >= 1)),
    )

    def send_terms(g):
        for part in range(2):
            xt[2 * g + part] = jnp.transpose(et[part]).astype(bf16)
        for level, ahead, cond in asides:
            @pl.when(cond)
            def _():
                term_aside(g, level, me + ahead).start()
        for level, cond in homes:
            @pl.when(cond & (me >= DISTANCES[level]))
            def _():
                term_home(g, level, me - DISTANCES[level]).start()

        def extra(i, _):
            @pl.when(me - gap_of(i) >= 0)
            def _():
                extra_term(g, i, me - gap_of(i)).start()
            return 0

        lax.fori_loop(0, len(FAR), extra, 0)

    def mix_terms(g):
        for level, cond in mixes:
            @pl.when(cond)
            def _():
                term_aside(g, level, me).wait_recv()
                tb[g, 2] = (tb[g, 2].astype(f32) + cr[g, level].astype(f32)).astype(bf16)

        @pl.when((col >= 2) & (row >= 1))
        def _():
            term_home(g, 2, me - 4).start()

    arrivals = (
        (0, (col <= 2) & (me + 1 < DEVICES)),
        (1, col <= 1),
        (2, me + 4 < DEVICES),
        (3, me + 8 < DEVICES),
    )

    def finish(g):
        for level, cond in arrivals:
            @pl.when(cond)
            def _():
                term_home(g, level, me).wait_recv()
                own[g] = own[g] + rb[g, level].astype(f32)

        def extra(i, _):
            @pl.when(me + gap_of(i) < DEVICES)
            def _():
                extra_term(g, i, me).wait_recv()
            return 0

        lax.fori_loop(0, len(FAR), extra, 0)
        for part, ref in enumerate((dk, dv)):
            folded = dot(spread[...], xr[2 * g + part], TN)
            ref[:, lanes(g)] = (jnp.transpose(own[g, part]) + folded).astype(bf16)

    lane = lax.broadcasted_iota(jnp.int32, (BLOCK, PAIR), 1)
    factor = math.log2(math.e) / math.sqrt(HD)
    scaling = 1.0 / math.sqrt(HD)

    def keys_of(g, c, part):
        if c == 0:
            return (k, v)[part][:, lanes(g)]
        if c < 5:
            return rx[g, c - 1, part]
        return xx[g, part]

    def forward(g, head):
        here = (lane // HD) == head
        query = q[:, lanes(g)]
        query = jnp.where(here, query, jnp.zeros_like(query))
        top = jnp.full((BLOCK, PAIR), very_negative, f32)
        for c, (low, size) in enumerate(CHUNKS):
            scores = dot(query, keys_of(g, c, 0), NT) * factor
            if c == 0:
                r = lax.broadcasted_iota(jnp.int32, (BLOCK, BLOCK), 0)
                j = lax.broadcasted_iota(jnp.int32, (BLOCK, BLOCK), 1)
                scores = jnp.where(r >= j, scores, very_negative)
            else:
                scores = scores + bias[0:1, low:low + size]
            s_ref[:, low:low + size] = scores
            for x in range(size // PAIR):
                top = jnp.maximum(top, scores[:, x * PAIR:(x + 1) * PAIR])
        top = jnp.max(top, axis=1, keepdims=True)
        total = jnp.zeros((BLOCK, PAIR), f32)
        mixed = jnp.zeros((HD, BLOCK), f32)
        features = pl.ds(pl.multiple_of(head * HD, HD), HD)
        for c, (low, size) in enumerate(CHUNKS):
            weights = jnp.exp2(s_ref[:, low:low + size] - top)
            for x in range(size // PAIR):
                total = total + weights[:, x * PAIR:(x + 1) * PAIR]
            weights = weights.astype(bf16)
            p_ref[:, low:low + size] = weights
            mixed = mixed + dot(vt[features, low:low + size], weights, NT)
        total = 1.0 / jnp.sum(total, axis=1, keepdims=True)
        mixed = jnp.transpose(mixed)
        mixed = jnp.concatenate([mixed, mixed], axis=1)
        mixed = (mixed * total).astype(bf16)
        grad = do[:, lanes(g)]
        grad = jnp.where(here, grad, jnp.zeros_like(grad)).astype(f32)
        delta = jnp.sum(grad * mixed.astype(f32), axis=1, keepdims=True) * total
        o[:, lanes(g)] = jnp.where(here, mixed, o[:, lanes(g)])
        return (grad * total).astype(bf16), delta

    def backward(g, head, grad, delta):
        here = (lane // HD) == head
        features = pl.ds(pl.multiple_of(head * HD, HD), HD)
        query_t = qt[g, features, :]
        dot_t[...] = jnp.transpose(grad.astype(f32)).astype(bf16)
        grad_t = dot_t[features, :]
        query_grad = jnp.zeros((BLOCK, PAIR), f32)
        for c, (low, size) in enumerate(CHUNKS):
            weight_grads = dot(grad, keys_of(g, c, 1), NT)
            weights = p_ref[:, low:low + size]
            score_grads = (weights.astype(f32) * (weight_grads - delta)).astype(bf16)
            query_grad = query_grad + dot(score_grads, keys_of(g, c, 0), NN)
            key_term = dot(query_t, score_grads, NN) * scaling
            value_term = dot(grad_t, weights, NN)
            for part, term in enumerate((key_term, value_term)):
                if c == 0:
                    own[g, part, features, :] = term
                elif c < 5:
                    tb[g, c - 1, part, features, :] = term.astype(bf16)
                else:
                    et[part, features, :] = term
        query_grad = (query_grad * scaling).astype(bf16)
        dq[:, lanes(g)] = jnp.where(here, query_grad, dq[:, lanes(g)])

    def transposed(a):
        return jnp.transpose(a.astype(f32)).astype(bf16)

    for g in range(GROUPS):
        qt[g] = transposed(q[:, g * PAIR:(g + 1) * PAIR])
    o[...] = jnp.zeros_like(o)
    dq[...] = jnp.zeros_like(dq)

    relay_blocks(0)

    def extras_arrive(i, _):
        @pl.when(me - gap_of(i) >= 0)
        def _():
            extra_copy(i, me).wait_recv()
        return 0

    def step(i, _):
        g = i // 2
        head = i % 2

        @pl.when(head == 0)
        def _():
            for level in (0, 1, 3):
                wait_blocks(g, level)

        @pl.when(i == 0)
        def _():
            lax.fori_loop(0, len(FAR), extras_arrive, 0)

        @pl.when(head == 0)
        def _():
            for c, (low, size) in enumerate(CHUNKS):
                vt[:, low:low + size] = transposed(keys_of(g, c, 1))

        grad, delta = forward(g, head)

        @pl.when((head == 0) & (g + 2 < GROUPS))
        def _():
            send_blocks(g + 2)

        @pl.when((head == 1) & (g + 1 < GROUPS))
        def _():
            relay_blocks(g + 1)

        @pl.when((head == 0) & (g >= 1))
        def _():
            mix_terms(g - 1)

        @pl.when((head == 1) & (g >= 2))
        def _():
            finish(g - 2)

        backward(g, head, grad, delta)

        @pl.when(head == 1)
        def _():
            send_terms(g)

        return 0

    lax.fori_loop(0, 2 * GROUPS, step, 0)
    mix_terms(GROUPS - 1)

    def last(g, _):
        finish(g)
        return 0

    lax.fori_loop(GROUPS - 2, GROUPS, last, 0)

    def extras_left(i, _):
        @pl.when(me + gap_of(i) < DEVICES)
        def _():
            extra_copy(i, me).wait_send()
        return 0

    lax.fori_loop(0, len(FAR), extras_left, 0)

    def left(g, _):
        for level, cond in direct:
            @pl.when(cond)
            def _():
                for copy in own_copies(g, level, me):
                    copy.wait_send()
        for level, back, cond in relays:
            @pl.when(cond)
            def _():
                for copy in relay_copies(g, level, me):
                    copy.wait_send()
        for level, distance in enumerate(DISTANCES):
            @pl.when(me >= distance)
            def _():
                term_home(g, level, me).wait_send()

        def extra(i, _):
            @pl.when(me - gap_of(i) >= 0)
            def _():
                extra_term(g, i, me).wait_send()
            return 0

        lax.fori_loop(0, len(FAR), extra, 0)
        return 0

    lax.fori_loop(0, GROUPS, left, 0)


def local(queries, key_rows, value_rows, grad_output, extra_blocks):
    whole = pl.BlockSpec(memory_space=pltpu.VMEM)
    slots = len(FAR)
    return pl.pallas_call(
        kernel,
        out_shape=[jax.ShapeDtypeStruct((BLOCK, WIDTH), bf16)] * 4,
        in_specs=[whole] * 4 + [pl.BlockSpec(memory_space=pltpu.SMEM)],
        out_specs=[whole] * 4,
        scratch_shapes=[
            pltpu.VMEM((GROUPS, 4, 2, BLOCK, PAIR), bf16),
            pltpu.VMEM((GROUPS, 2, EXTRA_ROWS, PAIR), bf16),
            pltpu.VMEM((GROUPS, 2, EXTRA_ROWS, PAIR), bf16),
            pltpu.VMEM((GROUPS, 4, 2, PAIR, BLOCK), bf16),
            pltpu.VMEM((GROUPS, 2, PAIR, BLOCK), f32),
            pltpu.VMEM((2, PAIR, EXTRA_ROWS), f32),
            pltpu.VMEM((2 * GROUPS, EXTRA_ROWS, PAIR), bf16),
            pltpu.VMEM((GROUPS, 4, 2, PAIR, BLOCK), bf16),
            pltpu.VMEM((GROUPS, 2, 2, PAIR, BLOCK), bf16),
            pltpu.VMEM((2 * GROUPS, EXTRA_ROWS, PAIR), bf16),
            pltpu.VMEM((BLOCK, KEYS), f32),
            pltpu.VMEM((BLOCK, KEYS), bf16),
            pltpu.VMEM((PAIR, KEYS), bf16),
            pltpu.VMEM((GROUPS, PAIR, BLOCK), bf16),
            pltpu.VMEM((PAIR, BLOCK), bf16),
            pltpu.VMEM((8, KEYS), f32),
            pltpu.VMEM((EXTRA_ROWS, BLOCK), bf16),
            pltpu.SemaphoreType.DMA((GROUPS, 4, 2)),
            pltpu.SemaphoreType.DMA((GROUPS, 4, 2)),
            pltpu.SemaphoreType.DMA((GROUPS, 4, 2)),
            pltpu.SemaphoreType.DMA((slots,)),
            pltpu.SemaphoreType.DMA((slots,)),
            pltpu.SemaphoreType.DMA((GROUPS, 4)),
            pltpu.SemaphoreType.DMA((GROUPS, 4)),
            pltpu.SemaphoreType.DMA((GROUPS, 4)),
            pltpu.SemaphoreType.DMA((GROUPS, slots)),
            pltpu.SemaphoreType.DMA((GROUPS, slots)),
        ],
        compiler_params=pltpu.CompilerParams(
            collective_id=0, has_side_effects=True, vmem_limit_bytes=60 << 20
        ),
    )(queries, key_rows, value_rows, grad_output, extra_blocks)


def solution(mesh):
    rows = P(("member", "tm"), None)
    return jax.shard_map(
        local,
        mesh=mesh,
        in_specs=(rows, rows, rows, rows, P("member", None)),
        out_specs=(rows, rows, rows, rows),
        check_vma=False,
    )
```

profile of v0, /device:TPU:48, one launch (start us, length us, event | category | flops | bytes accessed | tf_op | source)
XLA Modules:
  0.0 143.9 jit_solution(12954312481907450569)
XLA Ops:
  0.6 138.1 %shard_map.84 = (bf16[512,512]{1,0:T(8,128)(2,1)}, bf16[512,512]{1,0:T(8,128)(2,1)}, bf16[512,512]{1,0:T(8,128)(2,1)}, bf16[512,512]{1,0:T(8,128)(2,1)}) custom-call(bf16[512,512]{1,0:T(8,128)(2,1)} %q.1, bf16[512,512]{1,0:T(8,128)(2,1)} %k.1, bf16[512,512]{1,0:T(8,128)(2,1)} %v.1, bf16[512,512]{1,0:T(8,128)(2,1)} %do.1, s32[16,16]{1,0:T(8,128)} %table.1), custom_call_target="tpu_custom_call" | custom-call | tf_op jit(solution)/shard_map/pallas_call | solution.py:500
  138.8 0.0 copy-start.2
  138.8 1.9 %copy.13 = bf16[512,512]{1,0:T(8,128)(2,1)} copy(bf16[512,512]{1,0:T(8,128)(2,1)} %get-tuple-element.8) | data formatting | bytes 1048576
  140.7 0.0 copy-done.2
  140.7 0.0 copy-start.1
  140.7 0.8 copy.14
  141.5 0.4 copy-done.1
  141.9 0.0 copy-start
  141.9 0.8 copy.15
  142.7 0.4 copy-done
  143.2 0.8 copy.16
Async XLA Ops:
  138.8 1.9 %copy-start.2 = (bf16[512,512]{1,0:T(8,128)(2,1)S(1)}, bf16[512,512]{1,0:T(8,128)(2,1)}, u32[]{:S(2)}) copy-start(bf16[512,512]{1,0:T(8,128)(2,1)} %get-tuple-element.9) | copy-start | bytes 1572868
  140.7 1.2 copy-start.1
  141.9 1.2 copy-start
where the time goes:
time: 147 us; the launch traced here: 144 us
  Pallas kernels  138 us (94%)
  local copies, waits for them, and re-layouts  5.18 us (4%)
    pallas_call x1, Pallas kernels, local(): pl.pallas_call(kernel, out_shape=[jax.ShapeDtypeStruct((BLOCK, WIDTH), bf...  138 us
    unnamed x10, local copies, waits for them, and re-layouts  5.18 us

commit v1 on v0

--- a/solution.py
+++ b/solution.py
@@ -41,7 +41,7 @@
     q, k, v, do, table,
     o, dq, dk, dv,
     rx, xx, xs, tb, own, et, xt, rb, cr, xr,
-    s_ref, p_ref, vt, qt, dot_t, bias, spread,
+    p_far, p_own, o_own, stats, share_rows, qt, dt, bias, spread,
     send_kv, recv_kv, send_relay, send_x, recv_x,
     send_t, recv_t, recv_c, send_xt, recv_xt,
 ):
@@ -93,11 +93,11 @@
     )
 
     def send_blocks(g):
-        for level, cond in direct:
-            @pl.when(cond)
-            def _():
-                for copy in own_copies(g, level, me + DISTANCES[level]):
-                    copy.start()
+        for part in range(2):
+            for level, cond in direct:
+                @pl.when(cond)
+                def _():
+                    own_copies(g, level, me + DISTANCES[level])[part].start()
 
     def wait_blocks(g, level):
         @pl.when(me >= DISTANCES[level])
@@ -114,18 +114,17 @@
                     copy.start()
 
     send_blocks(0)
-    send_blocks(1)
 
     def gap_of(i):
         return i + 3 + (i + 10) // 11 + (i + 7) // 11
 
-    def extra_copy(i, to):
+    def extra_copy(g, i, to):
         rows = pl.ds(pl.multiple_of(i * SLOT_ROWS, SLOT_ROWS), SLOT_ROWS)
         return pltpu.make_async_remote_copy(
-            src_ref=xs.at[:, :, rows, :],
-            dst_ref=xx.at[:, :, rows, :],
-            send_sem=send_x.at[i],
-            recv_sem=recv_x.at[i],
+            src_ref=xs.at[g, :, rows, :],
+            dst_ref=xx.at[g, :, rows, :],
+            send_sem=send_x.at[g, i],
+            recv_sem=recv_x.at[g, i],
             device_id=device(to),
             device_id_type=MESH,
         )
@@ -163,13 +162,17 @@
         for g in range(GROUPS):
             xs[g, part] = dot(spread[...], ref[:, g * PAIR:(g + 1) * PAIR], NN).astype(bf16)
 
-    def extras_leave(i, _):
-        @pl.when(me + gap_of(i) < DEVICES)
-        def _():
-            extra_copy(i, me + gap_of(i)).start()
-        return 0
-
-    lax.fori_loop(0, len(FAR), extras_leave, 0)
+    def send_extras(g):
+        def one(i, _):
+            @pl.when(me + gap_of(i) < DEVICES)
+            def _():
+                extra_copy(g, i, me + gap_of(i)).start()
+            return 0
+
+        lax.fori_loop(0, len(FAR), one, 0)
+
+    relay_blocks(0)
+    send_extras(0)
 
     key_row = lax.broadcasted_iota(jnp.int32, (8, BLOCK), 1)
     for level, distance in enumerate(DISTANCES):
@@ -328,82 +331,144 @@
             return rx[g, c - 1, part]
         return xx[g, part]
 
+    def features_of(head):
+        return pl.ds(pl.multiple_of(head * HD, HD), HD)
+
+    def only(head, array):
+        return jnp.where((lane // HD) == head, array, jnp.zeros_like(array))
+
+    def folded_lanes(array, op):
+        result = array[:, :PAIR]
+        for x in range(1, array.shape[1] // PAIR):
+            result = op(result, array[:, x * PAIR:(x + 1) * PAIR])
+        return result
+
+    def attend(g, query, c):
+        low, size = CHUNKS[c]
+        scores = dot(query, keys_of(g, c, 0), NT) * factor
+        if c == 0:
+            r = lax.broadcasted_iota(jnp.int32, (BLOCK, BLOCK), 0)
+            j = lax.broadcasted_iota(jnp.int32, (BLOCK, BLOCK), 1)
+            scores = jnp.where(r >= j, scores, very_negative)
+        else:
+            scores = scores + bias[0:1, low:low + size]
+        top = jnp.max(folded_lanes(scores, jnp.maximum), axis=1, keepdims=True)
+        weights = jnp.exp2(scores - top)
+        total = jnp.sum(folded_lanes(weights, jnp.add), axis=1, keepdims=True)
+        weights = weights.astype(bf16)
+        return top, weights, total, dot(weights, keys_of(g, c, 1), NN)
+
+    def own_forward(i, _):
+        g, head = i // 2, i % 2
+        top, weights, total, mixed = attend(g, only(head, q[:, lanes(g)]), 0)
+        p_own[i] = weights
+        o_own[i] = mixed
+        stats[i] = jnp.where(lane == 0, top, total)
+        return 0
+
     def forward(g, head):
-        here = (lane // HD) == head
-        query = q[:, lanes(g)]
-        query = jnp.where(here, query, jnp.zeros_like(query))
-        top = jnp.full((BLOCK, PAIR), very_negative, f32)
-        for c, (low, size) in enumerate(CHUNKS):
-            scores = dot(query, keys_of(g, c, 0), NT) * factor
-            if c == 0:
-                r = lax.broadcasted_iota(jnp.int32, (BLOCK, BLOCK), 0)
-                j = lax.broadcasted_iota(jnp.int32, (BLOCK, BLOCK), 1)
-                scores = jnp.where(r >= j, scores, very_negative)
-            else:
-                scores = scores + bias[0:1, low:low + size]
-            s_ref[:, low:low + size] = scores
-            for x in range(size // PAIR):
-                top = jnp.maximum(top, scores[:, x * PAIR:(x + 1) * PAIR])
-        top = jnp.max(top, axis=1, keepdims=True)
-        total = jnp.zeros((BLOCK, PAIR), f32)
-        mixed = jnp.zeros((HD, BLOCK), f32)
-        features = pl.ds(pl.multiple_of(head * HD, HD), HD)
-        for c, (low, size) in enumerate(CHUNKS):
-            weights = jnp.exp2(s_ref[:, low:low + size] - top)
-            for x in range(size // PAIR):
-                total = total + weights[:, x * PAIR:(x + 1) * PAIR]
-            weights = weights.astype(bf16)
-            p_ref[:, low:low + size] = weights
-            mixed = mixed + dot(vt[features, low:low + size], weights, NT)
-        total = 1.0 / jnp.sum(total, axis=1, keepdims=True)
-        mixed = jnp.transpose(mixed)
-        mixed = jnp.concatenate([mixed, mixed], axis=1)
-        mixed = (mixed * total).astype(bf16)
-        grad = do[:, lanes(g)]
-        grad = jnp.where(here, grad, jnp.zeros_like(grad)).astype(f32)
-        delta = jnp.sum(grad * mixed.astype(f32), axis=1, keepdims=True) * total
-        o[:, lanes(g)] = jnp.where(here, mixed, o[:, lanes(g)])
-        return (grad * total).astype(bf16), delta
-
-    def backward(g, head, grad, delta):
-        here = (lane // HD) == head
-        features = pl.ds(pl.multiple_of(head * HD, HD), HD)
-        query_t = qt[g, features, :]
-        dot_t[...] = jnp.transpose(grad.astype(f32)).astype(bf16)
-        grad_t = dot_t[features, :]
+        i = 2 * g + head
+        query = only(head, q[:, lanes(g)])
+        tops, totals, mixes_ = [stats[i, :, 0:1]], [stats[i, :, 1:2]], [o_own[i]]
+        for c in range(1, 6):
+            low, size = CHUNKS[c]
+            top, weights, total, mixed = attend(g, query, c)
+            p_far[:, low - BLOCK:low - BLOCK + size] = weights
+            tops.append(top)
+            totals.append(total)
+            mixes_.append(mixed)
+        top = tops[0]
+        for c in range(1, 6):
+            top = jnp.maximum(top, tops[c])
+        shares = [jnp.exp2(x - top) for x in tops]
+        total = shares[0] * totals[0]
+        for c in range(1, 6):
+            total = total + shares[c] * totals[c]
+        total = 1.0 / total
+        shares = [share * total for share in shares]
+        mixed = mixes_[0] * shares[0]
+        for c in range(1, 6):
+            mixed = mixed + mixes_[c] * shares[c]
+        mixed = mixed.astype(bf16)
+        grad = only(head, do[:, lanes(g)]).astype(f32)
+        delta = jnp.sum(grad * mixed.astype(f32), axis=1, keepdims=True)
+        o[:, lanes(g)] = jnp.where((lane // HD) == head, mixed, o[:, lanes(g)])
+        columns = jnp.where(lane == 6, delta, 0.0)
+        for c in range(6):
+            columns = jnp.where(lane == c, shares[c], columns)
+        stats[i] = columns
+        share_rows[i] = jnp.transpose(columns)[0:8, :]
+
+    def differentiate(g, head, c, grad, columns, weights):
+        i = 2 * g + head
+        share = columns[:, c:c + 1]
+        keys = keys_of(g, c, 0)
+        scaled = (grad * share).astype(bf16)
+        scaled_t = (dt[g, features_of(head), :].astype(f32) * share_rows[i, c:c + 1, :]).astype(bf16)
+        weight_grads = dot(scaled, keys_of(g, c, 1), NT)
+        score_grads = (weights.astype(f32) * (weight_grads - columns[:, 6:7] * share)).astype(bf16)
+        half = BLOCK // 2
+        query_grad = jnp.concatenate(
+            [dot(score_grads[:half], keys, NN), dot(score_grads[half:], keys, NN)], axis=0
+        )
+        key_term = dot(qt[g, features_of(head), :], score_grads, NN) * scaling
+        return query_grad, key_term, dot(scaled_t, weights, NN)
+
+    def backward(g, head):
+        i = 2 * g + head
+        grad = only(head, do[:, lanes(g)]).astype(f32)
+        columns = stats[i]
+        features = features_of(head)
         query_grad = jnp.zeros((BLOCK, PAIR), f32)
-        for c, (low, size) in enumerate(CHUNKS):
-            weight_grads = dot(grad, keys_of(g, c, 1), NT)
-            weights = p_ref[:, low:low + size]
-            score_grads = (weights.astype(f32) * (weight_grads - delta)).astype(bf16)
-            query_grad = query_grad + dot(score_grads, keys_of(g, c, 0), NN)
-            key_term = dot(query_t, score_grads, NN) * scaling
-            value_term = dot(grad_t, weights, NN)
-            for part, term in enumerate((key_term, value_term)):
-                if c == 0:
-                    own[g, part, features, :] = term
-                elif c < 5:
+        for c in range(1, 6):
+            low, size = CHUNKS[c]
+            part_grad, *terms = differentiate(
+                g, head, c, grad, columns, p_far[:, low - BLOCK:low - BLOCK + size]
+            )
+            query_grad = query_grad + part_grad
+            for part, term in enumerate(terms):
+                if c < 5:
                     tb[g, c - 1, part, features, :] = term.astype(bf16)
                 else:
                     et[part, features, :] = term
-        query_grad = (query_grad * scaling).astype(bf16)
-        dq[:, lanes(g)] = jnp.where(here, query_grad, dq[:, lanes(g)])
+        o_own[i] = query_grad
+
+    def own_backward(i, _):
+        g, head = i // 2, i % 2
+        grad = only(head, do[:, lanes(g)]).astype(f32)
+        part_grad, *terms = differentiate(g, head, 0, grad, stats[i], p_own[i])
+        for part, term in enumerate(terms):
+            own[g, part, features_of(head), :] = term
+        query_grad = ((o_own[i] + part_grad) * scaling).astype(bf16)
+        dq[:, lanes(g)] = jnp.where((lane // HD) == head, query_grad, dq[:, lanes(g)])
+        return 0
 
     def transposed(a):
         return jnp.transpose(a.astype(f32)).astype(bf16)
 
     for g in range(GROUPS):
         qt[g] = transposed(q[:, g * PAIR:(g + 1) * PAIR])
+        dt[g] = transposed(do[:, g * PAIR:(g + 1) * PAIR])
     o[...] = jnp.zeros_like(o)
     dq[...] = jnp.zeros_like(dq)
 
-    relay_blocks(0)
-
-    def extras_arrive(i, _):
-        @pl.when(me - gap_of(i) >= 0)
-        def _():
-            extra_copy(i, me).wait_recv()
-        return 0
+    def own_forwards(g, _):
+        own_forward(2 * g, 0)
+        own_forward(2 * g + 1, 0)
+        return 0
+
+    lax.fori_loop(0, GROUPS, own_forwards, 0)
+    send_blocks(1)
+    send_extras(1)
+
+    def wait_extras(g):
+        def one(i, _):
+            @pl.when(me - gap_of(i) >= 0)
+            def _():
+                extra_copy(g, i, me).wait_recv()
+            return 0
+
+        lax.fori_loop(0, len(FAR), one, 0)
 
     def step(i, _):
         g = i // 2
@@ -413,36 +478,25 @@
         def _():
             for level in (0, 1, 3):
                 wait_blocks(g, level)
-
-        @pl.when(i == 0)
-        def _():
-            lax.fori_loop(0, len(FAR), extras_arrive, 0)
-
-        @pl.when(head == 0)
-        def _():
-            for c, (low, size) in enumerate(CHUNKS):
-                vt[:, low:low + size] = transposed(keys_of(g, c, 1))
-
-        grad, delta = forward(g, head)
+            wait_extras(g)
 
         @pl.when((head == 0) & (g + 2 < GROUPS))
         def _():
             send_blocks(g + 2)
-
-        @pl.when((head == 1) & (g + 1 < GROUPS))
+            send_extras(g + 2)
+
+        forward(g, head)
+
+        @pl.when((head == 0) & (g + 1 < GROUPS))
         def _():
             relay_blocks(g + 1)
 
-        @pl.when((head == 0) & (g >= 1))
+        backward(g, head)
+
+        @pl.when((head == 1) & (g >= 1))
         def _():
             mix_terms(g - 1)
 
-        @pl.when((head == 1) & (g >= 2))
-        def _():
-            finish(g - 2)
-
-        backward(g, head, grad, delta)
-
         @pl.when(head == 1)
         def _():
             send_terms(g)
@@ -450,21 +504,20 @@
         return 0
 
     lax.fori_loop(0, 2 * GROUPS, step, 0)
+
+    def own_backwards(g, _):
+        own_backward(2 * g, 0)
+        own_backward(2 * g + 1, 0)
+        return 0
+
+    lax.fori_loop(0, GROUPS, own_backwards, 0)
     mix_terms(GROUPS - 1)
 
     def last(g, _):
         finish(g)
         return 0
 
-    lax.fori_loop(GROUPS - 2, GROUPS, last, 0)
-
-    def extras_left(i, _):
-        @pl.when(me + gap_of(i) < DEVICES)
-        def _():
-            extra_copy(i, me).wait_send()
-        return 0
-
-    lax.fori_loop(0, len(FAR), extras_left, 0)
+    lax.fori_loop(0, GROUPS, last, 0)
 
     def left(g, _):
         for level, cond in direct:
@@ -483,6 +536,10 @@
                 term_home(g, level, me).wait_send()
 
         def extra(i, _):
+            @pl.when(me + gap_of(i) < DEVICES)
+            def _():
+                extra_copy(g, i, me).wait_send()
+
             @pl.when(me - gap_of(i) >= 0)
             def _():
                 extra_term(g, i, me).wait_send()
@@ -492,12 +549,17 @@
         return 0
 
     lax.fori_loop(0, GROUPS, left, 0)
+
+
+def publish(*refs):
+    for i in range(4):
+        refs[i + 4][...] = refs[i][...]
 
 
 def local(queries, key_rows, value_rows, grad_output, extra_blocks):
     whole = pl.BlockSpec(memory_space=pltpu.VMEM)
     slots = len(FAR)
-    return pl.pallas_call(
+    results = pl.pallas_call(
         kernel,
         out_shape=[jax.ShapeDtypeStruct((BLOCK, WIDTH), bf16)] * 4,
         in_specs=[whole] * 4 + [pl.BlockSpec(memory_space=pltpu.SMEM)],
@@ -513,18 +575,20 @@
             pltpu.VMEM((GROUPS, 4, 2, PAIR, BLOCK), bf16),
             pltpu.VMEM((GROUPS, 2, 2, PAIR, BLOCK), bf16),
             pltpu.VMEM((2 * GROUPS, EXTRA_ROWS, PAIR), bf16),
-            pltpu.VMEM((BLOCK, KEYS), f32),
-            pltpu.VMEM((BLOCK, KEYS), bf16),
-            pltpu.VMEM((PAIR, KEYS), bf16),
+            pltpu.VMEM((BLOCK, KEYS - BLOCK), bf16),
+            pltpu.VMEM((2 * GROUPS, BLOCK, BLOCK), bf16),
+            pltpu.VMEM((2 * GROUPS, BLOCK, PAIR), f32),
+            pltpu.VMEM((2 * GROUPS, BLOCK, PAIR), f32),
+            pltpu.VMEM((2 * GROUPS, 8, BLOCK), f32),
             pltpu.VMEM((GROUPS, PAIR, BLOCK), bf16),
-            pltpu.VMEM((PAIR, BLOCK), bf16),
+            pltpu.VMEM((GROUPS, PAIR, BLOCK), bf16),
             pltpu.VMEM((8, KEYS), f32),
             pltpu.VMEM((EXTRA_ROWS, BLOCK), bf16),
             pltpu.SemaphoreType.DMA((GROUPS, 4, 2)),
             pltpu.SemaphoreType.DMA((GROUPS, 4, 2)),
             pltpu.SemaphoreType.DMA((GROUPS, 4, 2)),
-            pltpu.SemaphoreType.DMA((slots,)),
-            pltpu.SemaphoreType.DMA((slots,)),
+            pltpu.SemaphoreType.DMA((GROUPS, slots)),
+            pltpu.SemaphoreType.DMA((GROUPS, slots)),
             pltpu.SemaphoreType.DMA((GROUPS, 4)),
             pltpu.SemaphoreType.DMA((GROUPS, 4)),
             pltpu.SemaphoreType.DMA((GROUPS, 4)),
@@ -535,6 +599,14 @@
             collective_id=0, has_side_effects=True, vmem_limit_bytes=60 << 20
         ),
     )(queries, key_rows, value_rows, grad_output, extra_blocks)
+    rows = pl.BlockSpec((BLOCK // 4, WIDTH), lambda i: (i, 0))
+    return pl.pallas_call(
+        publish,
+        grid=(4,),
+        out_shape=[jax.ShapeDtypeStruct((BLOCK, WIDTH), bf16)] * 4,
+        in_specs=[rows] * 4,
+        out_specs=[rows] * 4,
+    )(*results)
 
 
 def solution(mesh):

time: 147 us -> 130 us (0.88); the launches traced: 144 us -> 130 us
  Pallas kernels: 138 us -> 129 us
  local copies, waits for them, and re-layouts: 5.18 us -> 0 us
    pallas_call x1, Pallas kernels: 138 us -> 125 us  [local(): pl.pallas_call(kernel, out_shape=[jax.ShapeDtypeStruct((BLOCK, WIDTH), bf...]
    unnamed x10 -> x0, local copies, waits for them, and re-layouts: 5.18 us -> none
    pallas_call x0 -> x1, Pallas kernels: none -> 3.81 us  [local(): pl.pallas_call(publish, grid=(4,), out_shape=[jax.ShapeDtypeStruct((BLOCK...]
where the time goes in v1:
time: 130 us
  Pallas kernels  129 us (99%)
    pallas_call x1, Pallas kernels, local(): pl.pallas_call(kernel, out_shape=[jax.ShapeDtypeStruct((BLOCK, WIDTH), bf...  125 us
    pallas_call x1, Pallas kernels, local(): pl.pallas_call(publish, grid=(4,), out_shape=[jax.ShapeDtypeStruct((BLOCK...  3.81 us

profile of v1, /device:TPU:48, one launch (start us, length us, event | category | flops | bytes accessed | tf_op | source)
XLA Modules:
  0.0 129.8 jit_solution(13499927107366445855)
XLA Ops:
  0.6 125.4 %shard_map.84 = (bf16[512,512]{1,0:T(8,128)(2,1)}, bf16[512,512]{1,0:T(8,128)(2,1)}, bf16[512,512]{1,0:T(8,128)(2,1)}, bf16[512,512]{1,0:T(8,128)(2,1)}) custom-call(bf16[512,512]{1,0:T(8,128)(2,1)} %q.1, bf16[512,512]{1,0:T(8,128)(2,1)} %k.1, bf16[512,512]{1,0:T(8,128)(2,1)} %v.1, bf16[512,512]{1,0:T(8,128)(2,1)} %do.1, s32[16,16]{1,0:T(8,128)} %table.1), custom_call_target="tpu_custom_call" | custom-call | tf_op jit(solution)/shard_map/pallas_call | solution.py:562
  126.0 3.8 %shard_map.85 = (bf16[512,512]{1,0:T(8,128)(2,1)}, bf16[512,512]{1,0:T(8,128)(2,1)}, bf16[512,512]{1,0:T(8,128)(2,1)}, bf16[512,512]{1,0:T(8,128)(2,1)}) custom-call(bf16[512,512]{1,0:T(8,128)(2,1)} %get-tuple-element.8.refs_0_, bf16[512,512]{1,0:T(8,128)(2,1)} %get-tuple-element.9.refs_1_, bf16[512,512]{1,0:T(8,128)(2,1)} %get-tuple-element.10.refs_2_, ...), custom_call_target="tpu_custom_call" | custom-call | tf_op jit(solution)/shard_map/pallas_call | solution.py:603

commit v2 on v1

--- a/solution.py
+++ b/solution.py
@@ -28,6 +28,7 @@
 DISTANCES = (1, 2, 4, 8)
 FAR = tuple(d for d in range(1, DEVICES) if d not in DISTANCES)
 SLOT_ROWS = CAP * SUB
+LAG = 2
 EXTRA_ROWS = 384
 KEYS = 5 * BLOCK + EXTRA_ROWS
 CHUNKS = tuple((i * BLOCK, BLOCK) for i in range(5)) + ((5 * BLOCK, EXTRA_ROWS),)
@@ -85,35 +86,46 @@
         (2, me + 4 < DEVICES),
         (0, (col < 3) & (me + 1 < DEVICES)),
         (1, col < 2),
-        (3, me + 8 < DEVICES),
     )
+    farthest = (3, me + 8 < DEVICES)
     relays = (
         (0, 3, (col == 3) & (row >= 1)),
         (1, 2, (col >= 2) & (row >= 1)),
     )
 
+    def send_part(g, part, targets):
+        for level, cond in targets:
+            @pl.when(cond)
+            def _():
+                own_copies(g, level, me + DISTANCES[level])[part].start()
+
     def send_blocks(g):
         for part in range(2):
-            for level, cond in direct:
-                @pl.when(cond)
-                def _():
-                    own_copies(g, level, me + DISTANCES[level])[part].start()
+            send_part(g, part, direct)
+
+    def wait_part(g, level, part):
+        @pl.when(me >= DISTANCES[level])
+        def _():
+            own_copies(g, level, me)[part].wait_recv()
 
     def wait_blocks(g, level):
-        @pl.when(me >= DISTANCES[level])
-        def _():
-            for copy in own_copies(g, level, me):
-                copy.wait_recv()
-
-    def relay_blocks(g):
-        wait_blocks(g, 2)
+        for part in range(2):
+            wait_part(g, level, part)
+
+    def relay_part(g, part):
+        wait_part(g, 2, part)
         for level, back, cond in relays:
             @pl.when(cond)
             def _():
-                for copy in relay_copies(g, level, me - back):
-                    copy.start()
-
-    send_blocks(0)
+                relay_copies(g, level, me - back)[part].start()
+
+    def relay_blocks(g):
+        for part in range(2):
+            relay_part(g, part)
+        for part in range(2):
+            send_part(g, part, (farthest,))
+
+    send_part(0, 0, direct)
 
     def gap_of(i):
         return i + 3 + (i + 10) // 11 + (i + 7) // 11
@@ -171,8 +183,8 @@
 
         lax.fori_loop(0, len(FAR), one, 0)
 
-    relay_blocks(0)
-    send_extras(0)
+    relay_part(0, 0)
+    send_part(0, 1, direct)
 
     key_row = lax.broadcasted_iota(jnp.int32, (8, BLOCK), 1)
     for level, distance in enumerate(DISTANCES):
@@ -221,21 +233,25 @@
 
     lax.fori_loop(0, len(FAR), clear_extra, 0)
 
-    def term_copy(g, level, dst, recv, to):
+    def term_rows(i):
+        return i // 2, pl.ds(pl.multiple_of((i % 2) * HD, HD), HD)
+
+    def term_copy(i, level, place, recv, to):
+        g, rows = term_rows(i)
         return pltpu.make_async_remote_copy(
-            src_ref=tb.at[g, level],
-            dst_ref=dst,
-            send_sem=send_t.at[g, level],
-            recv_sem=recv,
+            src_ref=tb.at[g, level, :, rows, :],
+            dst_ref=place.at[g, level, :, rows, :],
+            send_sem=send_t.at[i, level],
+            recv_sem=recv.at[i, level],
             device_id=device(to),
             device_id_type=MESH,
         )
 
-    def term_home(g, level, to):
-        return term_copy(g, level, rb.at[g, level], recv_t.at[g, level], to)
-
-    def term_aside(g, level, to):
-        return term_copy(g, level, cr.at[g, level], recv_c.at[g, level], to)
+    def term_home(i, level, to):
+        return term_copy(i, level, rb, recv_t, to)
+
+    def term_aside(i, level, to):
+        return term_copy(i, level, cr, recv_c, to)
 
     def extra_term(g, i, to):
         rows = pl.ds(pl.multiple_of(i * SLOT_ROWS, SLOT_ROWS), SLOT_ROWS)
@@ -264,17 +280,19 @@
         (1, (col >= 2) & (row >= 1)),
     )
 
-    def send_terms(g):
+    def send_terms(i):
+        for level, ahead, cond in asides:
+            @pl.when(cond)
+            def _():
+                term_aside(i, level, me + ahead).start()
+        for level, cond in homes:
+            @pl.when(cond & (me >= DISTANCES[level]))
+            def _():
+                term_home(i, level, me - DISTANCES[level]).start()
+
+    def send_extra_terms(g):
         for part in range(2):
             xt[2 * g + part] = jnp.transpose(et[part]).astype(bf16)
-        for level, ahead, cond in asides:
-            @pl.when(cond)
-            def _():
-                term_aside(g, level, me + ahead).start()
-        for level, cond in homes:
-            @pl.when(cond & (me >= DISTANCES[level]))
-            def _():
-                term_home(g, level, me - DISTANCES[level]).start()
 
         def extra(i, _):
             @pl.when(me - gap_of(i) >= 0)
@@ -284,16 +302,19 @@
 
         lax.fori_loop(0, len(FAR), extra, 0)
 
-    def mix_terms(g):
+    def mix_terms(i):
+        g, rows = term_rows(i)
         for level, cond in mixes:
             @pl.when(cond)
             def _():
-                term_aside(g, level, me).wait_recv()
-                tb[g, 2] = (tb[g, 2].astype(f32) + cr[g, level].astype(f32)).astype(bf16)
+                term_aside(i, level, me).wait_recv()
+                tb[g, 2, :, rows, :] = (
+                    tb[g, 2, :, rows, :].astype(f32) + cr[g, level, :, rows, :].astype(f32)
+                ).astype(bf16)
 
         @pl.when((col >= 2) & (row >= 1))
         def _():
-            term_home(g, 2, me - 4).start()
+            term_home(i, 2, me - 4).start()
 
     arrivals = (
         (0, (col <= 2) & (me + 1 < DEVICES)),
@@ -306,7 +327,8 @@
         for level, cond in arrivals:
             @pl.when(cond)
             def _():
-                term_home(g, level, me).wait_recv()
+                term_home(2 * g, level, me).wait_recv()
+                term_home(2 * g + 1, level, me).wait_recv()
                 own[g] = own[g] + rb[g, level].astype(f32)
 
         def extra(i, _):
@@ -457,9 +479,12 @@
         own_forward(2 * g + 1, 0)
         return 0
 
-    lax.fori_loop(0, GROUPS, own_forwards, 0)
-    send_blocks(1)
-    send_extras(1)
+    lax.fori_loop(0, GROUPS // 2, own_forwards, 0)
+    relay_part(0, 1)
+    for part in range(2):
+        send_part(0, part, (farthest,))
+    send_extras(0)
+    lax.fori_loop(GROUPS // 2, GROUPS, own_forwards, 0)
 
     def wait_extras(g):
         def one(i, _):
@@ -480,26 +505,28 @@
                 wait_blocks(g, level)
             wait_extras(g)
 
-        @pl.when((head == 0) & (g + 2 < GROUPS))
-        def _():
-            send_blocks(g + 2)
-            send_extras(g + 2)
+        @pl.when((head == 0) & (g + 1 < GROUPS))
+        def _():
+            send_blocks(g + 1)
 
         forward(g, head)
 
-        @pl.when((head == 0) & (g + 1 < GROUPS))
+        @pl.when((head == 1) & (g + 1 < GROUPS))
         def _():
             relay_blocks(g + 1)
+            send_extras(g + 1)
 
         backward(g, head)
 
-        @pl.when((head == 1) & (g >= 1))
-        def _():
-            mix_terms(g - 1)
+        @pl.when(i >= LAG)
+        def _():
+            mix_terms(i - LAG)
+
+        send_terms(i)
 
         @pl.when(head == 1)
         def _():
-            send_terms(g)
+            send_extra_terms(g)
 
         return 0
 
@@ -510,8 +537,14 @@
         own_backward(2 * g + 1, 0)
         return 0
 
-    lax.fori_loop(0, GROUPS, own_backwards, 0)
-    mix_terms(GROUPS - 1)
+    lax.fori_loop(0, GROUPS // 2, own_backwards, 0)
+
+    def late_mix(i, _):
+        mix_terms(i)
+        return 0
+
+    lax.fori_loop(2 * GROUPS - LAG, 2 * GROUPS, late_mix, 0)
+    lax.fori_loop(GROUPS // 2, GROUPS, own_backwards, 0)
 
     def last(g, _):
         finish(g)
@@ -520,7 +553,7 @@
     lax.fori_loop(0, GROUPS, last, 0)
 
     def left(g, _):
-        for level, cond in direct:
+        for level, cond in direct + (farthest,):
             @pl.when(cond)
             def _():
                 for copy in own_copies(g, level, me):
@@ -533,7 +566,8 @@
         for level, distance in enumerate(DISTANCES):
             @pl.when(me >= distance)
             def _():
-                term_home(g, level, me).wait_send()
+                term_home(2 * g, level, me).wait_send()
+                term_home(2 * g + 1, level, me).wait_send()
 
         def extra(i, _):
             @pl.when(me + gap_of(i) < DEVICES)
@@ -589,9 +623,9 @@
             pltpu.SemaphoreType.DMA((GROUPS, 4, 2)),
             pltpu.SemaphoreType.DMA((GROUPS, slots)),
             pltpu.SemaphoreType.DMA((GROUPS, slots)),
-            pltpu.SemaphoreType.DMA((GROUPS, 4)),
-            pltpu.SemaphoreType.DMA((GROUPS, 4)),
-            pltpu.SemaphoreType.DMA((GROUPS, 4)),
+            pltpu.SemaphoreType.DMA((2 * GROUPS, 4)),
+            pltpu.SemaphoreType.DMA((2 * GROUPS, 4)),
+            pltpu.SemaphoreType.DMA((2 * GROUPS, 4)),
             pltpu.SemaphoreType.DMA((GROUPS, slots)),
             pltpu.SemaphoreType.DMA((GROUPS, slots)),
         ],
@@ -599,13 +633,11 @@
             collective_id=0, has_side_effects=True, vmem_limit_bytes=60 << 20
         ),
     )(queries, key_rows, value_rows, grad_output, extra_blocks)
-    rows = pl.BlockSpec((BLOCK // 4, WIDTH), lambda i: (i, 0))
     return pl.pallas_call(
         publish,
-        grid=(4,),
         out_shape=[jax.ShapeDtypeStruct((BLOCK, WIDTH), bf16)] * 4,
-        in_specs=[rows] * 4,
-        out_specs=[rows] * 4,
+        in_specs=[whole] * 4,
+        out_specs=[whole] * 4,
     )(*results)
 
 

time: 130 us -> 116 us (0.89)
  Pallas kernels: 129 us -> 114 us
    pallas_call x1, Pallas kernels: 125 us -> 111 us  [local(): pl.pallas_call(kernel, out_shape=[jax.ShapeDtypeStruct((BLOCK, WIDTH), bf...]
where the time goes in v2:
time: 116 us; the launch traced here: 115 us
  Pallas kernels  114 us (98%)
    pallas_call x1, Pallas kernels, local(): pl.pallas_call(kernel, out_shape=[jax.ShapeDtypeStruct((BLOCK, WIDTH), bf...  111 us
    pallas_call x1, Pallas kernels, local(): pl.pallas_call(publish, out_shape=[jax.ShapeDtypeStruct((BLOCK, WIDTH), b...  2.86 us

profile of v2, /device:TPU:48, one launch (start us, length us, event | category | flops | bytes accessed | tf_op | source)
XLA Modules:
  0.0 114.8 jit_solution(11217164598471795631)
XLA Ops:
  0.6 111.3 %shard_map.84 = (bf16[512,512]{1,0:T(8,128)(2,1)}, bf16[512,512]{1,0:T(8,128)(2,1)}, bf16[512,512]{1,0:T(8,128)(2,1)}, bf16[512,512]{1,0:T(8,128)(2,1)}) custom-call(bf16[512,512]{1,0:T(8,128)(2,1)} %q.1, bf16[512,512]{1,0:T(8,128)(2,1)} %k.1, bf16[512,512]{1,0:T(8,128)(2,1)} %v.1, bf16[512,512]{1,0:T(8,128)(2,1)} %do.1, s32[16,16]{1,0:T(8,128)} %table.1), custom_call_target="tpu_custom_call" | custom-call | tf_op jit(solution)/shard_map/pallas_call | solution.py:596
  111.9 2.9 %shard_map.85 = (bf16[512,512]{1,0:T(8,128)(2,1)}, bf16[512,512]{1,0:T(8,128)(2,1)}, bf16[512,512]{1,0:T(8,128)(2,1)}, bf16[512,512]{1,0:T(8,128)(2,1)}) custom-call(bf16[512,512]{1,0:T(8,128)(2,1)} %get-tuple-element.8.refs_0_, bf16[512,512]{1,0:T(8,128)(2,1)} %get-tuple-element.9.refs_1_, bf16[512,512]{1,0:T(8,128)(2,1)} %get-tuple-element.10.refs_2_, ...), custom_call_target="tpu_custom_call" | custom-call | tf_op jit(solution)/shard_map/pallas_call | solution.py:636

commit v3 on v2

--- a/solution.py
+++ b/solution.py
@@ -82,11 +82,12 @@
     def relay_copies(g, level, to):
         return kv_copies(g, level, rx.at[g, 2, 0], rx.at[g, 2, 1], send_relay, to)
 
-    direct = (
-        (2, me + 4 < DEVICES),
+    relayed = ((2, me + 4 < DEVICES),)
+    nearest = (
         (0, (col < 3) & (me + 1 < DEVICES)),
         (1, col < 2),
     )
+    direct = relayed + nearest
     farthest = (3, me + 8 < DEVICES)
     relays = (
         (0, 3, (col == 3) & (row >= 1)),
@@ -99,9 +100,9 @@
             def _():
                 own_copies(g, level, me + DISTANCES[level])[part].start()
 
-    def send_blocks(g):
+    def send_both(g, targets):
         for part in range(2):
-            send_part(g, part, direct)
+            send_part(g, part, targets)
 
     def wait_part(g, level, part):
         @pl.when(me >= DISTANCES[level])
@@ -122,8 +123,6 @@
     def relay_blocks(g):
         for part in range(2):
             relay_part(g, part)
-        for part in range(2):
-            send_part(g, part, (farthest,))
 
     send_part(0, 0, direct)
 
@@ -481,10 +480,10 @@
 
     lax.fori_loop(0, GROUPS // 2, own_forwards, 0)
     relay_part(0, 1)
-    for part in range(2):
-        send_part(0, part, (farthest,))
+    send_both(0, (farthest,))
     send_extras(0)
     lax.fori_loop(GROUPS // 2, GROUPS, own_forwards, 0)
+    send_both(1, relayed)
 
     def wait_extras(g):
         def one(i, _):
@@ -507,14 +506,16 @@
 
         @pl.when((head == 0) & (g + 1 < GROUPS))
         def _():
-            send_blocks(g + 1)
+            send_both(g + 1, nearest)
+            relay_blocks(g + 1)
+            send_both(g + 1, (farthest,))
+            send_extras(g + 1)
 
         forward(g, head)
 
-        @pl.when((head == 1) & (g + 1 < GROUPS))
-        def _():
-            relay_blocks(g + 1)
-            send_extras(g + 1)
+        @pl.when((head == 1) & (g + 2 < GROUPS))
+        def _():
+            send_both(g + 2, relayed)
 
         backward(g, head)
 

time: 116 us -> 114 us (0.983)
  Pallas kernels: 114 us -> 112 us
    pallas_call x1, Pallas kernels: 111 us -> 109 us  [local(): pl.pallas_call(kernel, out_shape=[jax.ShapeDtypeStruct((BLOCK, WIDTH), bf...]
where the time goes in v3:
time: 114 us; the launch traced here: 113 us
  Pallas kernels  112 us (98%)
    pallas_call x1, Pallas kernels, local(): pl.pallas_call(kernel, out_shape=[jax.ShapeDtypeStruct((BLOCK, WIDTH), bf...  109 us
    pallas_call x1, Pallas kernels, local(): pl.pallas_call(publish, out_shape=[jax.ShapeDtypeStruct((BLOCK, WIDTH), b...  2.86 us

profile of v3, /device:TPU:48, one launch (start us, length us, event | category | flops | bytes accessed | tf_op | source)
XLA Modules:
  0.0 112.9 jit_solution(14336288293187881936)
XLA Ops:
  0.6 109.4 %shard_map.84 = (bf16[512,512]{1,0:T(8,128)(2,1)}, bf16[512,512]{1,0:T(8,128)(2,1)}, bf16[512,512]{1,0:T(8,128)(2,1)}, bf16[512,512]{1,0:T(8,128)(2,1)}) custom-call(bf16[512,512]{1,0:T(8,128)(2,1)} %q.1, bf16[512,512]{1,0:T(8,128)(2,1)} %k.1, bf16[512,512]{1,0:T(8,128)(2,1)} %v.1, bf16[512,512]{1,0:T(8,128)(2,1)} %do.1, s32[16,16]{1,0:T(8,128)} %table.1), custom_call_target="tpu_custom_call" | custom-call | tf_op jit(solution)/shard_map/pallas_call | solution.py:597
  110.0 2.9 %shard_map.85 = (bf16[512,512]{1,0:T(8,128)(2,1)}, bf16[512,512]{1,0:T(8,128)(2,1)}, bf16[512,512]{1,0:T(8,128)(2,1)}, bf16[512,512]{1,0:T(8,128)(2,1)}) custom-call(bf16[512,512]{1,0:T(8,128)(2,1)} %get-tuple-element.8.refs_0_, bf16[512,512]{1,0:T(8,128)(2,1)} %get-tuple-element.9.refs_1_, bf16[512,512]{1,0:T(8,128)(2,1)} %get-tuple-element.10.refs_2_, ...), custom_call_target="tpu_custom_call" | custom-call | tf_op jit(solution)/shard_map/pallas_call | solution.py:637

commit v4 on v3

--- a/solution.py
+++ b/solution.py
@@ -284,10 +284,14 @@
             @pl.when(cond)
             def _():
                 term_aside(i, level, me + ahead).start()
+        send_homes(i, (0, 1))
+
+    def send_homes(i, levels):
         for level, cond in homes:
-            @pl.when(cond & (me >= DISTANCES[level]))
-            def _():
-                term_home(i, level, me - DISTANCES[level]).start()
+            if level in levels:
+                @pl.when(cond & (me >= DISTANCES[level]))
+                def _():
+                    term_home(i, level, me - DISTANCES[level]).start()
 
     def send_extra_terms(g):
         for part in range(2):
@@ -452,6 +456,8 @@
                     tb[g, c - 1, part, features, :] = term.astype(bf16)
                 else:
                     et[part, features, :] = term
+            if c == 2:
+                send_terms(i)
         o_own[i] = query_grad
 
     def own_backward(i, _):
@@ -498,6 +504,10 @@
         g = i // 2
         head = i % 2
 
+        @pl.when(i >= LAG)
+        def _():
+            own_backward(i - LAG, 0)
+
         @pl.when(head == 0)
         def _():
             for level in (0, 1, 3):
@@ -507,9 +517,9 @@
         @pl.when((head == 0) & (g + 1 < GROUPS))
         def _():
             send_both(g + 1, nearest)
+            send_extras(g + 1)
             relay_blocks(g + 1)
             send_both(g + 1, (farthest,))
-            send_extras(g + 1)
 
         forward(g, head)
 
@@ -523,7 +533,7 @@
         def _():
             mix_terms(i - LAG)
 
-        send_terms(i)
+        send_homes(i, (2, 3))
 
         @pl.when(head == 1)
         def _():
@@ -533,19 +543,12 @@
 
     lax.fori_loop(0, 2 * GROUPS, step, 0)
 
-    def own_backwards(g, _):
-        own_backward(2 * g, 0)
-        own_backward(2 * g + 1, 0)
-        return 0
-
-    lax.fori_loop(0, GROUPS // 2, own_backwards, 0)
-
-    def late_mix(i, _):
+    def ending(i, _):
         mix_terms(i)
-        return 0
-
-    lax.fori_loop(2 * GROUPS - LAG, 2 * GROUPS, late_mix, 0)
-    lax.fori_loop(GROUPS // 2, GROUPS, own_backwards, 0)
+        own_backward(i, 0)
+        return 0
+
+    lax.fori_loop(2 * GROUPS - LAG, 2 * GROUPS, ending, 0)
 
     def last(g, _):
         finish(g)

time: 114 us -> 115 us (level)
    pallas_call x1, Pallas kernels: 109 us -> 111 us  [local(): pl.pallas_call(kernel, out_shape=[jax.ShapeDtypeStruct((BLOCK, WIDTH), bf...]
where the time goes in v4:
time: 115 us; the launch traced here: 114 us
  Pallas kernels  113 us (98%)
    pallas_call x1, Pallas kernels, local(): pl.pallas_call(kernel, out_shape=[jax.ShapeDtypeStruct((BLOCK, WIDTH), bf...  111 us
    pallas_call x1, Pallas kernels, local(): pl.pallas_call(publish, out_shape=[jax.ShapeDtypeStruct((BLOCK, WIDTH), b...  2.86 us

profile of v4, /device:TPU:48, one launch (start us, length us, event | category | flops | bytes accessed | tf_op | source)
XLA Modules:
  0.0 114.1 jit_solution(8959309200880404028)
XLA Ops:
  0.6 110.6 %shard_map.84 = (bf16[512,512]{1,0:T(8,128)(2,1)}, bf16[512,512]{1,0:T(8,128)(2,1)}, bf16[512,512]{1,0:T(8,128)(2,1)}, bf16[512,512]{1,0:T(8,128)(2,1)}) custom-call(bf16[512,512]{1,0:T(8,128)(2,1)} %q.1, bf16[512,512]{1,0:T(8,128)(2,1)} %k.1, bf16[512,512]{1,0:T(8,128)(2,1)} %v.1, bf16[512,512]{1,0:T(8,128)(2,1)} %do.1, s32[16,16]{1,0:T(8,128)} %table.1), custom_call_target="tpu_custom_call" | custom-call | tf_op jit(solution)/shard_map/pallas_call | solution.py:600
  111.2 2.9 %shard_map.85 = (bf16[512,512]{1,0:T(8,128)(2,1)}, bf16[512,512]{1,0:T(8,128)(2,1)}, bf16[512,512]{1,0:T(8,128)(2,1)}, bf16[512,512]{1,0:T(8,128)(2,1)}) custom-call(bf16[512,512]{1,0:T(8,128)(2,1)} %get-tuple-element.8.refs_0_, bf16[512,512]{1,0:T(8,128)(2,1)} %get-tuple-element.9.refs_1_, bf16[512,512]{1,0:T(8,128)(2,1)} %get-tuple-element.10.refs_2_, ...), custom_call_target="tpu_custom_call" | custom-call | tf_op jit(solution)/shard_map/pallas_call | solution.py:640
